TPU v7x, 256 devices: a whole 4x4x8 slice. The times are simulated.
256 devices in a mesh: row: 64 (over y, z, core), col: 4 (over x).
Axes of the slice: x: 4, y: 4, z: 8, core: 2. Of those that a mesh axis runs over, the one named last changes fastest.
Arguments:
- factor: float32 [8192, 8192], P('row', 'col'), may hold values from -0.125 to 0.125
- rhs: float32 [8192, 512], P('row', 'col'), may hold values from -6 to 6
- parent: int32 [7], replicated, may hold values from 4 to 6, as said below
- bounds: int32 [8], replicated, may hold values from 0 to 64, as said below
- slot: int32 [64], replicated, may hold values from 0 to 63, each once
- structure: int32 [7, 64], replicated, may hold values 0 or 1
Outputs:
- solution: float32 [8192, 512], P('row', 'col')
Inputs may be any that keep to these rules, and one draw needn't show every extreme that they name: parent[s] is 4 or 5 for s = 0 to 3, and 6 for s = 4, 5, 6 (the root is its own entry). bounds[0] = 0, bounds[7] = 64, strictly increasing; supernode s holds logical blocks bounds[s] to bounds[s+1] - 1. `slot`: a permutation.
All inputs are finite; a program needn't handle non-finite values.
Results may differ from a plain program's by a relative error of at most 0.0001.
Values sent between devices are 32-bit elements; how exact they have to be, the bound alone decides.
A program may use at most 64 MiB of HBM per device.

v0:
```python
import jax
import jax.numpy as jnp
from jax import lax
from jax.sharding import PartitionSpec as P

B = 128
RB = 1


def block_masks(parent, bounds, slot, structure):
    count = slot.shape[0]
    ar = jnp.arange(count, dtype=jnp.int32)
    logical = jnp.sum(jnp.where(slot[:, None] == ar[None, :], ar[:, None], 0), axis=0)
    node = jnp.sum((logical[:, None] >= bounds[None, 1:7]).astype(jnp.int32), axis=1)
    level = (node >= 4).astype(jnp.int32) + (node >= 6).astype(jnp.int32)
    nodes = jnp.arange(7, dtype=jnp.int32)
    grand = parent[parent]
    ancestor = ((nodes[None, :] == parent[:, None]) | (nodes[None, :] == grand[:, None])) & (
        nodes[None, :] != nodes[:, None]
    )
    node_hot = (node[:, None] == nodes[None, :]).astype(jnp.float32)
    perm_hot = (logical[:, None] == ar[None, :]).astype(jnp.float32)
    listed_store = jnp.dot(
        structure.astype(jnp.float32), perm_hot.T, precision=lax.Precision.HIGHEST
    )
    anc_pairs = jnp.dot(
        node_hot,
        jnp.dot(ancestor.astype(jnp.float32), node_hot.T, precision=lax.Precision.HIGHEST),
        precision=lax.Precision.HIGHEST,
    )
    list_pairs = jnp.dot(node_hot, listed_store, precision=lax.Precision.HIGHEST)
    link = (anc_pairs * list_pairs).T > 0.5
    same = node[:, None] == node[None, :]
    return (level, same, link)


def masked(block_rows, mask):
    rblocks, width = mask.shape
    bsz = block_rows.shape[0] // rblocks
    shaped = block_rows.reshape(rblocks, bsz, width, bsz) * mask[:, None, :, None].astype(
        jnp.float32
    )
    return shaped.reshape(block_rows.shape)


def body(factor, rhs, parent, bounds, slot, structure):
    level, same, link = block_masks(parent, bounds, slot, structure)
    first = lax.axis_index("row") * RB
    level_mine = lax.dynamic_slice_in_dim(level, first, RB, 0)
    same_mine = lax.dynamic_slice_in_dim(same, first, RB, 0)
    link_mine = lax.dynamic_slice_in_dim(link, first, RB, 0)
    full_rows = lax.all_gather(factor, "col", axis=1, tiled=True)
    diag_part = masked(full_rows, same_mine)
    link_part = masked(full_rows, link_mine)

    def product(matrix, vector):
        return jnp.dot(
            matrix,
            lax.all_gather(vector, "row", axis=0, tiled=True),
            precision=lax.Precision.HIGHEST,
            preferred_element_type=jnp.float32,
        )

    pieces = [rhs]
    accums = [jnp.zeros(p.shape, jnp.float32) for p in pieces]
    results = [jnp.zeros(p.shape, jnp.float32) for p in pieces]
    for section in range(3):
        rows = jnp.repeat(level_mine == section, B)[:, None]
        solved = jnp.where(rows, product(diag_part, pieces[0] - accums[0]), 0.0)
        results[0] = results[0] + solved
        if section < 2:
            accums[0] = accums[0] + product(link_part, solved)
    return results[0]


def solution(mesh):
    in_specs = (P("row", "col"), P("row", "col"), P(), P(), P(), P())
    out_specs = P("row", "col")
    return jax.shard_map(body, mesh=mesh, in_specs=in_specs, out_specs=out_specs, check_vma=False)
```

profile of v0, /device:TPU:1, one launch (start us, length us, event | category | flops | bytes accessed | tf_op | source)
XLA Modules:
  0.0 501.4 jit_solution(158808282834339269)
XLA Ops:
  6.5 0.0 all-gather.7.cloned.1.call-start
  6.5 0.7 all-gather.7.cloned.1.call-update
  7.3 0.0 all-gather.9.cloned.1.call-start
  7.3 0.7 all-gather.9.cloned.1.call-update
  8.0 0.0 all-gather.11.cloned.1.call-start
  8.1 0.7 slice.3
  8.8 0.7 select_reduce_fusion
  9.5 0.1 convert_reduce_fusion
  9.6 0.6 dynamic-slice
  10.2 0.7 dynamic_slice.9
  11.6 0.7 fusion.48
  12.2 0.1 broadcast_bitcast_fusion.1
  12.3 51.4 %all-gather.7.cloned.1.call-done = f32[128,8192]{1,0:T(8,128)} async-done(((f32[128,2048]{1,0:T(8,128)}), f32[128,8192]{1,0:T(8,128)}) %all-gather.7.cloned.1.call-update) | async-done | bytes 4194320 | tf_op jit(solution)/shard_map/all_gather | solution.py:52
  63.8 82.7 %all-gather.9.cloned.1.call-done = f32[8192,128]{1,0:T(8,128)} async-done(((f32[128,128]{1,0:T(8,128)}), f32[8192,128]{1,0:T(8,128)}) %all-gather.9.cloned.1.call-update) | async-done | bytes 4194320 | tf_op jit(solution)/shard_map/all_gather | solution.py:59
  146.5 0.0 copy-start
  146.5 0.0 copy-start.4
  146.5 0.0 copy-start.1
  146.5 8.4 %fusion.15 = f32[128,128]{1,0:T(8,128)} fusion(f32[8192,128]{1,0:T(8,128)} %all-gather.9.cloned.1.call-done, f32[128,8192]{1,0:T(8,128)} %all-gather.7.cloned.1.call-done, f32[8192]{0:T(1024)S(1)} %broadcast_bitcast_fusion.1, pred[]{:T(512)} %bitcast), kind=kOutput, calls=%fused_computation.16 | convolution fusion | flops 1611677696 | bytes 8486913 | tf_op jit(solution)/shard_map/dot_general | solution.py:57
  154.9 0.0 all-gather.11.cloned.1.call-update
  154.9 0.0 all-gather.13.cloned.1.call-start
  155.0 0.0 copy-done
  155.0 0.6 gather_fusion
  155.6 0.2 fusion.35
  155.8 0.0 copy-done.4
  155.8 0.2 fusion.36
  156.0 0.3 fusion.33
  156.3 0.2 fusion.34
  156.6 0.1 broadcast_bitcast_fusion
  156.7 74.7 %all-gather.11.cloned.1.call-done = f32[8192,128]{1,0:T(8,128)} async-done(((f32[128,128]{1,0:T(8,128)}), f32[8192,128]{1,0:T(8,128)}) %all-gather.11.cloned.1.call-update) | async-done | bytes 4194320 | tf_op jit(solution)/shard_map/all_gather | solution.py:59
  231.4 0.0 copy-done.1
  231.4 8.4 %fusion.50 = (f32[128,128]{1,0:T(8,128)}, f32[128,128]{1,0:T(8,128)S(1)}) fusion(f32[128,128]{1,0:T(8,128)S(1)} %copy-done.1, f32[8192,128]{1,0:T(8,128)} %all-gather.11.cloned.1.call-done, f32[128,8192]{1,0:T(8,128)} %all-gather.7.cloned.1.call-done, f32[8192]{0:T(1024)S(1)} %broadcast_bitcast_fusion), kind=kOutput, calls=%fused_computation.55 | convolution fusion | flops 1611677696 | bytes 8617984 | tf_op jit(solution)/shard_map/dot_general | solution.py:57
  239.8 0.0 all-gather.13.cloned.1.call-update
  239.8 0.2 all-gather.15.cloned.1.call-start
  240.7 75.6 %all-gather.13.cloned.1.call-done = f32[8192,128]{1,0:T(8,128)} async-done(((f32[128,128]{1,0:T(8,128)}), f32[8192,128]{1,0:T(8,128)}) %all-gather.13.cloned.1.call-update) | async-done | bytes 4194320 | tf_op jit(solution)/shard_map/all_gather | solution.py:59
  316.3 8.4 %fusion.18 = f32[128,128]{1,0:T(8,128)} fusion(f32[8192,128]{1,0:T(8,128)} %all-gather.13.cloned.1.call-done, f32[128,8192]{1,0:T(8,128)} %all-gather.7.cloned.1.call-done, f32[8192]{0:T(1024)S(1)} %broadcast_bitcast_fusion.1, pred[]{:T(512)} %bitcast.3), kind=kOutput, calls=%fused_computation.17 | convolution fusion | flops 1611677696 | bytes 8486913 | tf_op jit(solution)/shard_map/dot_general | solution.py:57
  324.7 0.0 all-gather.15.cloned.1.call-update
  324.7 0.0 all-gather.17.cloned.1.call-start
  324.8 76.4 %all-gather.15.cloned.1.call-done = f32[8192,128]{1,0:T(8,128)} async-done(((f32[128,128]{1,0:T(8,128)}), f32[8192,128]{1,0:T(8,128)}) %all-gather.15.cloned.1.call-update) | async-done | bytes 4194320 | tf_op jit(solution)/shard_map/all_gather | solution.py:59
  401.2 0.0 copy-start.2
  401.2 0.0 copy-start.3
  401.2 8.4 %fusion.30 = f32[128,128]{1,0:T(8,128)} fusion(f32[128,128]{1,0:T(8,128)S(1)} %copy-done.1, f32[128,128]{1,0:T(8,128)S(1)} %get-tuple-element.6, f32[8192,128]{1,0:T(8,128)} %all-gather.15.cloned.1.call-done, f32[128,8192]{1,0:T(8,128)} %all-gather.7.cloned.1.call-done, f32[8192]{0:T(1024)S(1)} %broadcast_bitcast_fusion), kind=kOutput, calls=%fused_computation.21 | convolution fusion | flops 1611694080 | bytes 8617984 | tf_op jit(solution)/shard_map/dot_general | solution.py:57
  409.6 0.0 all-gather.17.cloned.1.call-update
  410.3 75.8 %all-gather.17.cloned.1.call-done = f32[8192,128]{1,0:T(8,128)} async-done(((f32[128,128]{1,0:T(8,128)}), f32[8192,128]{1,0:T(8,128)}) %all-gather.17.cloned.1.call-update) | async-done | bytes 4194320 | tf_op jit(solution)/shard_map/all_gather | solution.py:59
  486.1 0.0 copy-done.2
  486.1 0.0 copy-done.3
  486.1 8.4 %fusion.24 = f32[128,128]{1,0:T(8,128)} fusion(f32[8192,128]{1,0:T(8,128)} %all-gather.17.cloned.1.call-done, f32[128,8192]{1,0:T(8,128)} %all-gather.7.cloned.1.call-done, f32[8192]{0:T(1024)S(1)} %broadcast_bitcast_fusion.1, f32[128,128]{1,0:T(8,128)S(1)} %copy-done.2, f32[128,128]{1,0:T(8,128)S(1)} %copy-done.3, pred[]{:T(512)} %bitcast.6), kind=kOutput, calls=%fused_computation.19 | convolution fusion | flops 1611710464 | bytes 8617985 | tf_op jit(solution)/shard_map/dot_general | solution.py:57
  (4 shorter events, 0.0 us)
Async XLA Ops:
  6.5 57.2 %all-gather.7.cloned.1.call-start = ((), (), s32[]{:S(2)}) async-start(), calls=%async_computation | async-start | bytes 5242880 | tf_op jit(solution)/shard_map/all_gather | solution.py:52
  7.3 139.2 %all-gather.9.cloned.1.call-start = ((), (), s32[]{:S(2)}) async-start(), calls=%async_computation.1 | async-start | bytes 4259840 | tf_op jit(solution)/shard_map/all_gather | solution.py:59
  8.0 223.4 %all-gather.11.cloned.1.call-start = ((), (), s32[]{:S(2)}) async-start(), calls=%async_computation.2 | async-start | bytes 4259840 | tf_op jit(solution)/shard_map/all_gather | solution.py:59
  146.5 8.5 %copy-start = (s32[7]{0:T(128)S(1)}, s32[7]{0:T(128)}, u32[]{:S(2)}) copy-start(s32[7]{0:T(128)} %param.8) | copy-start | bytes 88
  146.5 9.4 %copy-start.4 = (s32[7,64]{1,0:T(8,128)S(1)}, s32[7,64]{1,0:T(8,128)}, u32[]{:S(2)}) copy-start(s32[7,64]{1,0:T(8,128)} %param.11) | copy-start | bytes 5380
  146.5 84.9 %copy-start.1 = (f32[128,128]{1,0:T(8,128)S(1)}, f32[128,128]{1,0:T(8,128)}, u32[]{:S(2)}) copy-start(f32[128,128]{1,0:T(8,128)} %param.7) | copy-start | bytes 196612
  154.9 161.4 %all-gather.13.cloned.1.call-start = ((), (), s32[]{:S(2)}) async-start(), calls=%async_computation.3 | async-start | bytes 4259840 | tf_op jit(solution)/shard_map/all_gather | solution.py:59
  239.8 161.4 %all-gather.15.cloned.1.call-start = ((), (), s32[]{:S(2)}) async-start(), calls=%async_computation.4 | async-start | bytes 4259840 | tf_op jit(solution)/shard_map/all_gather | solution.py:59
  324.7 161.4 %all-gather.17.cloned.1.call-start = ((), (), s32[]{:S(2)}) async-start(), calls=%async_computation.5 | async-start | bytes 4259840 | tf_op jit(solution)/shard_map/all_gather | solution.py:59
  401.2 84.9 %copy-start.2 = (f32[128,128]{1,0:T(8,128)S(1)}, f32[128,128]{1,0:T(8,128)}, u32[]{:S(2)}) copy-start(f32[128,128]{1,0:T(8,128)} %fusion.15) | copy-start | bytes 196612
  401.2 84.9 %copy-start.3 = (f32[128,128]{1,0:T(8,128)S(1)}, f32[128,128]{1,0:T(8,128)}, u32[]{:S(2)}) copy-start(f32[128,128]{1,0:T(8,128)} %fusion.18) | copy-start | bytes 196612
Sparse Core Ops, SparseCore 0:
  9.2 54.5 all-gather.6
  66.5 79.8 all-gather.8
  155.0 76.3 all-gather.10
  239.9 76.3 all-gather.12
  324.8 76.3 all-gather.14
  409.8 76.3 all-gather.16
where the time goes:
time: 501 us
  waiting for transfers between devices  438 us (87%)
  matrix products  42.9 us (9%)
  between operations  15.6 us (3%)
    all_gather x5, waiting for transfers between devices, product(): lax.all_gather(vector, 'row', axis=0, tiled=True)  385 us
    all_gather x1, waiting for transfers between devices, body(): full_rows = lax.all_gather(factor, 'col', axis=1, tiled=True)  51.4 us
    dot_general x5, matrix products, product(): jnp.dot(matrix, lax.all_gather(vector, 'row', axis=0, tiled=True), precis...  42 us
  transfers between devices with their start and end apart: 6, of which 6 were waited for; matrix products, arithmetic and copies ran while one was open for 1% of the time, Pallas kernels for 0%

commit v1 on v0

--- a/solution.py
+++ b/solution.py
@@ -1,3 +1,4 @@
+import functools
 import jax
 import jax.numpy as jnp
 from jax import lax
@@ -5,6 +6,39 @@
 
 B = 128
 RB = 1
+
+
+def patch_clear(inputs, axis_key):
+    block_last, passed, p_next = (
+        jax.lax.psum(1, axis_key),
+        jax.lax.axis_index(axis_key),
+        inputs.shape[1],
+    )
+    fields = [jj * block_last if dev_i == 1 else jj for dev_i, jj in enumerate(inputs.shape)]
+    r2 = lax.dynamic_update_slice_in_dim(
+        jnp.zeros(fields, inputs.dtype), inputs, passed * p_next, axis=1
+    )
+    side_arr = long_array = inputs
+    for num in range(1, block_last // 2 + 1):
+        side_arr = jax.lax.ppermute(
+            side_arr, axis_key, [(dev_i, (dev_i + 1) % block_last) for dev_i in range(block_last)]
+        )
+        r2 = lax.dynamic_update_slice_in_dim(
+            r2, side_arr, (passed - num) % block_last * p_next, axis=1
+        )
+        if 2 * num < block_last:
+            long_array = jax.lax.ppermute(
+                long_array,
+                axis_key,
+                [(dev_i, (dev_i - 1) % block_last) for dev_i in range(block_last)],
+            )
+            r2 = lax.dynamic_update_slice_in_dim(
+                r2, long_array, (passed + num) % block_last * p_next, axis=1
+            )
+    return r2
+
+
+sites_choose = functools.partial(patch_clear, axis_key="col")
 
 
 def block_masks(parent, bounds, slot, structure):
@@ -49,7 +83,7 @@
     level_mine = lax.dynamic_slice_in_dim(level, first, RB, 0)
     same_mine = lax.dynamic_slice_in_dim(same, first, RB, 0)
     link_mine = lax.dynamic_slice_in_dim(link, first, RB, 0)
-    full_rows = lax.all_gather(factor, "col", axis=1, tiled=True)
+    full_rows = sites_choose(factor)
     diag_part = masked(full_rows, same_mine)
     link_part = masked(full_rows, link_mine)
 

time: 501 us -> 448 us (0.89)
  waiting for transfers between devices: 438 us -> 372 us
  local copies, waits for them, and re-layouts: 2.79 us -> 10.7 us
  starting transfers between devices: 0.38 us -> 5.93 us
    all_gather x1 -> x0, waiting for transfers between devices: 51.4 us -> none  [body(): full_rows = lax.all_gather(factor, 'col', axis=1, tiled=True)]
    all_gather x5, waiting for transfers between devices: 385 us -> 338 us  [product(): lax.all_gather(vector, 'row', axis=0, tiled=True)]
    ppermute x0 -> x3, waiting for transfers between devices: none -> 32.9 us  [the longest x2 32.9 us: patch_clear(): jax.lax.ppermute(side_arr, axis_key, [(dev_i, (dev_i + 1) % block_last) f...]
    dynamic_update_slice x0 -> x4, local copies, waits for them, and re-layouts: none -> 5.49 us  [the longest x2 3.4 us: patch_clear(): lax.dynamic_update_slice_in_dim(r2, side_arr, (passed - num) % block_last...]
    ppermute x0 -> x3, starting transfers between devices: none -> 5.36 us  [the longest x2 4.01 us: patch_clear(): jax.lax.ppermute(side_arr, axis_key, [(dev_i, (dev_i + 1) % block_last) f...]
  transfers between devices with their start and end apart: 6 -> 8, of which waited for: 6 -> 7; matrix products, arithmetic and copies ran while one was open for 1% -> 3% of each run, Pallas kernels for 0% -> 0%
where the time goes in v1:
time: 448 us
  waiting for transfers between devices  372 us (83%)
  matrix products  42.9 us (10%)
  between operations  15.3 us (3%)
  local copies, waits for them, and re-layouts  10.7 us (2%)
  starting transfers between devices  5.93 us (1%)
    all_gather x5, waiting for transfers between devices, product(): lax.all_gather(vector, 'row', axis=0, tiled=True)  338 us
    dot_general x5, matrix products, product(): jnp.dot(matrix, lax.all_gather(vector, 'row', axis=0, tiled=True), precis...  42 us
    ppermute x2, waiting for transfers between devices, patch_clear(): jax.lax.ppermute(side_arr, axis_key, [(dev_i, (dev_i + 1) % block_last) f...  32.9 us
  transfers between devices with their start and end apart: 8, of which 7 were waited for; matrix products, arithmetic and copies ran while one was open for 3% of the time, Pallas kernels for 0%

profile of v1, /device:TPU:1, one launch (start us, length us, event | category | flops | bytes accessed | tf_op | source)
XLA Modules:
  0.0 448.0 jit_solution(2574681358208293760)
XLA Ops:
  6.5 0.0 all-gather.6.cloned.1.call-start
  6.5 0.7 all-gather.6.cloned.1.call-update
  7.3 0.0 all-gather.8.cloned.1.call-start
  7.3 2.1 collective-permute-start
  9.4 1.4 collective-permute-start.1
  10.8 0.7 slice.3
  11.5 0.7 select_reduce_fusion
  12.3 0.1 convert_reduce_fusion
  12.3 0.6 dynamic-slice
  12.9 18.6 %collective-permute-done = f32[128,2048]{1,0:T(8,128)S(1)} collective-permute-done((f32[128,2048]{1,0:T(8,128)}, f32[128,2048]{1,0:T(8,128)S(1)}, u32[]{:S(2)}, u32[]{:S(2)}) %collective-permute-start) | collective-permute-done | bytes 1048608 | tf_op jit(solution)/shard_map/ppermute | solution.py:23
  31.5 1.9 collective-permute-start.2
  33.4 0.6 fusion.48
  34.1 0.7 dynamic_slice.9
  35.5 0.1 broadcast_bitcast_fusion.1
  35.5 2.4 broadcast_in_dim.67
  38.0 0.0 copy-done.1
  38.0 1.1 constant_dynamic-update-slice_fusion.3
  39.0 1.1 constant_dynamic-update-slice_fusion.2
  40.1 0.0 collective-permute-done.1
  40.1 1.0 constant_dynamic-update-slice_fusion.1
  41.1 14.4 %collective-permute-done.2 = f32[128,2048]{1,0:T(8,128)} collective-permute-done((f32[128,2048]{1,0:T(8,128)S(1)}, f32[128,2048]{1,0:T(8,128)}, u32[]{:S(2)}, u32[]{:S(2)}) %collective-permute-start.2) | collective-permute-done | bytes 1048608 | tf_op jit(solution)/shard_map/ppermute | solution.py:23
  55.5 2.3 constant_dynamic-update-slice_fusion
  57.8 35.6 %all-gather.6.cloned.1.call-done = f32[8192,128]{1,0:T(8,128)} async-done(((f32[128,128]{1,0:T(8,128)}), f32[8192,128]{1,0:T(8,128)}) %all-gather.6.cloned.1.call-update) | async-done | bytes 4194320 | tf_op jit(solution)/shard_map/all_gather | solution.py:93
  93.4 8.4 %fusion.15 = f32[128,128]{1,0:T(8,128)} fusion(f32[8192,128]{1,0:T(8,128)} %all-gather.6.cloned.1.call-done, f32[128,8192]{1,0:T(8,128)} %constant_dynamic-update-slice_fusion, f32[8192]{0:T(1024)S(1)} %broadcast_bitcast_fusion.1, pred[]{:T(512)} %bitcast), kind=kOutput, calls=%fused_computation.16 | convolution fusion | flops 1611677696 | bytes 8486913 | tf_op jit(solution)/shard_map/dot_general | solution.py:91
  101.9 0.0 all-gather.8.cloned.1.call-update
  101.9 0.2 all-gather.10.cloned.1.call-start
  102.1 0.0 copy-done
  102.2 0.6 gather_fusion
  102.8 0.2 fusion.32
  103.0 0.0 copy-done.5
  103.0 0.2 fusion.35
  103.2 0.3 fusion.31
  103.5 0.2 fusion.30
  103.7 0.1 broadcast_bitcast_fusion
  103.8 74.6 %all-gather.8.cloned.1.call-done = f32[8192,128]{1,0:T(8,128)} async-done(((f32[128,128]{1,0:T(8,128)}), f32[8192,128]{1,0:T(8,128)}) %all-gather.8.cloned.1.call-update) | async-done | bytes 4194320 | tf_op jit(solution)/shard_map/all_gather | solution.py:93
  178.4 0.0 copy-done.2
  178.4 8.4 %fusion.50 = (f32[128,128]{1,0:T(8,128)}, f32[128,128]{1,0:T(8,128)S(1)}) fusion(f32[128,128]{1,0:T(8,128)S(1)} %copy-done.2, f32[8192,128]{1,0:T(8,128)} %all-gather.8.cloned.1.call-done, f32[128,8192]{1,0:T(8,128)} %constant_dynamic-update-slice_fusion, f32[8192]{0:T(1024)S(1)} %broadcast_bitcast_fusion), kind=kOutput, calls=%fused_computation.61 | convolution fusion | flops 1611677696 | bytes 8617984 | tf_op jit(solution)/shard_map/dot_general | solution.py:91
  186.8 0.0 all-gather.10.cloned.1.call-update
  186.8 0.0 all-gather.12.cloned.1.call-start
  187.5 75.7 %all-gather.10.cloned.1.call-done = f32[8192,128]{1,0:T(8,128)} async-done(((f32[128,128]{1,0:T(8,128)}), f32[8192,128]{1,0:T(8,128)}) %all-gather.10.cloned.1.call-update) | async-done | bytes 4194320 | tf_op jit(solution)/shard_map/all_gather | solution.py:93
  263.3 8.4 %fusion.18 = f32[128,128]{1,0:T(8,128)} fusion(f32[8192,128]{1,0:T(8,128)} %all-gather.10.cloned.1.call-done, f32[128,8192]{1,0:T(8,128)} %constant_dynamic-update-slice_fusion, f32[8192]{0:T(1024)S(1)} %broadcast_bitcast_fusion.1, pred[]{:T(512)} %bitcast.3), kind=kOutput, calls=%fused_computation.17 | convolution fusion | flops 1611677696 | bytes 8486913 | tf_op jit(solution)/shard_map/dot_general | solution.py:91
  271.6 0.0 all-gather.12.cloned.1.call-update
  271.7 0.3 all-gather.14.cloned.1.call-start
  271.9 76.2 %all-gather.12.cloned.1.call-done = f32[8192,128]{1,0:T(8,128)} async-done(((f32[128,128]{1,0:T(8,128)}), f32[8192,128]{1,0:T(8,128)}) %all-gather.12.cloned.1.call-update) | async-done | bytes 4194320 | tf_op jit(solution)/shard_map/all_gather | solution.py:93
  348.1 8.4 %fusion.27 = f32[128,128]{1,0:T(8,128)} fusion(f32[128,128]{1,0:T(8,128)S(1)} %copy-done.2, f32[128,128]{1,0:T(8,128)S(1)} %get-tuple-element.6, f32[8192,128]{1,0:T(8,128)} %all-gather.12.cloned.1.call-done, f32[128,8192]{1,0:T(8,128)} %constant_dynamic-update-slice_fusion, f32[8192]{0:T(1024)S(1)} %broadcast_bitcast_fusion), kind=kOutput, calls=%fused_computation.20 | convolution fusion | flops 1611694080 | bytes 8617984 | tf_op jit(solution)/shard_map/dot_general | solution.py:91
  356.5 0.0 all-gather.14.cloned.1.call-update
  357.3 75.8 %all-gather.14.cloned.1.call-done = f32[8192,128]{1,0:T(8,128)} async-done(((f32[128,128]{1,0:T(8,128)}), f32[8192,128]{1,0:T(8,128)}) %all-gather.14.cloned.1.call-update) | async-done | bytes 4194320 | tf_op jit(solution)/shard_map/all_gather | solution.py:93
  433.1 8.4 %add_add_fusion = f32[128,128]{1,0:T(8,128)} fusion(f32[128,128]{1,0:T(8,128)S(1)} %copy-done.3, f32[128,128]{1,0:T(8,128)S(1)} %copy-done.4, f32[8192,128]{1,0:T(8,128)} %all-gather.14.cloned.1.call-done, f32[128,8192]{1,0:T(8,128)} %constant_dynamic-update-slice_fusion, f32[8192]{0:T(1024)S(1)} %broadcast_bitcast_fusion.1, pred[]{:T(512)} %bitcast.6), kind=kOutput, calls=%fused_computation.21 | convolution fusion | flops 1611710464 | bytes 8617985 | tf_op jit(solution)/shard_map/dot_general | solution.py:91
  (12 shorter events, 0.0 us)
Async XLA Ops:
  6.5 31.4 %copy-start.1 = (f32[128,2048]{1,0:T(8,128)S(1)}, f32[128,2048]{1,0:T(8,128)}, u32[]{:S(2)}) copy-start(f32[128,2048]{1,0:T(8,128)} %param.6) | copy-start | bytes 3145732
  6.5 86.9 %all-gather.6.cloned.1.call-start = ((), (), s32[]{:S(2)}) async-start(), calls=%async_computation | async-start | bytes 4259840 | tf_op jit(solution)/shard_map/all_gather | solution.py:93
  7.3 171.1 %all-gather.8.cloned.1.call-start = ((), (), s32[]{:S(2)}) async-start(), calls=%async_computation.1 | async-start | bytes 4259840 | tf_op jit(solution)/shard_map/all_gather | solution.py:93
  7.3 24.2 %collective-permute-start = (f32[128,2048]{1,0:T(8,128)}, f32[128,2048]{1,0:T(8,128)S(1)}, u32[]{:S(2)}, u32[]{:S(2)}) collective-permute-start(f32[128,2048]{1,0:T(8,128)} %param.6), channel_id=1, source_target_pairs={{0,1},{1,2},{2,3},{3,0},{4,5},{5,6},{6,7},{7,4},{8,9},{9,10},{10,1... | collective-permute-start | bytes 3145736 | tf_op jit(solution)/shard_map/ppermute | solution.py:23
  9.4 30.7 %collective-permute-start.1 = (f32[128,2048]{1,0:T(8,128)}, f32[128,2048]{1,0:T(8,128)S(1)}, u32[]{:S(2)}, u32[]{:S(2)}) collective-permute-start(f32[128,2048]{1,0:T(8,128)} %param.6), channel_id=1, source_target_pairs={{0,3},{1,0},{2,1},{3,2},{4,7},{5,4},{6,5},{7,6},{8,11},{9,8},{10,9... | collective-permute-start | bytes 3145736 | tf_op jit(solution)/shard_map/ppermute | solution.py:30
  31.5 24.0 %collective-permute-start.2 = (f32[128,2048]{1,0:T(8,128)S(1)}, f32[128,2048]{1,0:T(8,128)}, u32[]{:S(2)}, u32[]{:S(2)}) collective-permute-start(f32[128,2048]{1,0:T(8,128)S(1)} %collective-permute-done), channel_id=1, source_target_pairs={{0,1},{1,2},{2,3},{3,0},{4,5},{5,6},{6,7},{7,4},{8,9},{9,10},{10,1... | collective-permute-start | bytes 3145736 | tf_op jit(solution)/shard_map/ppermute | solution.py:23
  93.4 8.7 %copy-start = (s32[7]{0:T(128)S(1)}, s32[7]{0:T(128)}, u32[]{:S(2)}) copy-start(s32[7]{0:T(128)} %param.8) | copy-start | bytes 88
  93.4 9.6 %copy-start.5 = (s32[7,64]{1,0:T(8,128)S(1)}, s32[7,64]{1,0:T(8,128)}, u32[]{:S(2)}) copy-start(s32[7,64]{1,0:T(8,128)} %param.11) | copy-start | bytes 5380
  93.4 84.9 %copy-start.2 = (f32[128,128]{1,0:T(8,128)S(1)}, f32[128,128]{1,0:T(8,128)}, u32[]{:S(2)}) copy-start(f32[128,128]{1,0:T(8,128)} %param.7) | copy-start | bytes 196612
  101.9 161.4 %all-gather.10.cloned.1.call-start = ((), (), s32[]{:S(2)}) async-start(), calls=%async_computation.2 | async-start | bytes 4259840 | tf_op jit(solution)/shard_map/all_gather | solution.py:93
  186.8 161.4 %all-gather.12.cloned.1.call-start = ((), (), s32[]{:S(2)}) async-start(), calls=%async_computation.3 | async-start | bytes 4259840 | tf_op jit(solution)/shard_map/all_gather | solution.py:93
  271.7 161.4 %all-gather.14.cloned.1.call-start = ((), (), s32[]{:S(2)}) async-start(), calls=%async_computation.4 | async-start | bytes 4259840 | tf_op jit(solution)/shard_map/all_gather | solution.py:93
  348.1 84.9 %copy-start.3 = (f32[128,128]{1,0:T(8,128)S(1)}, f32[128,128]{1,0:T(8,128)}, u32[]{:S(2)}) copy-start(f32[128,128]{1,0:T(8,128)} %fusion.15) | copy-start | bytes 196612
  348.1 84.9 %copy-start.4 = (f32[128,128]{1,0:T(8,128)S(1)}, f32[128,128]{1,0:T(8,128)}, u32[]{:S(2)}) copy-start(f32[128,128]{1,0:T(8,128)} %fusion.18) | copy-start | bytes 196612
Sparse Core Ops, SparseCore 0:
  10.1 83.2 all-gather.5
  102.0 76.3 all-gather.7
  186.9 76.3 all-gather.9
  271.8 76.3 all-gather.11
  356.7 76.3 all-gather.13
